TPU v7x, 256 devices: a whole 4x4x8 slice. The times are simulated.
256 devices in a mesh: row: 8 (over y, z_lo), col: 32 (over z_hi, x, core).
Axes of the slice: x: 4, y: 4, z: 8 (z_hi: 4, z_lo: 2; z = z_hi * 2 + z_lo), core: 2. Of those that a mesh axis runs over, the one named last changes fastest.
Arguments:
- grad_output: bfloat16 [1024, 8192], P('col', 'row'), may hold values from -6 to 6
- inputs: bfloat16 [1024, 28672], P('row', 'col'), may hold values from -0.1875 to 0.1875
- weight: bfloat16 [28672, 8192], P('col', 'row'), may hold values from -0.125 to 0.125
- block_mask: int32 [224, 64], P('col'), may hold values from 0 to 1, as said below
Outputs:
- grad_input: bfloat16 [1024, 28672], P('row', 'col')
- grad_weight: bfloat16 [28672, 8192], P('col', 'row')
Inputs may be any that keep to these rules, and one draw needn't show every extreme that they name: `block_mask`: 1 where the 128 x 128 block of weight is kept, 0 where it is zero; the share of kept blocks differs widely from block row to block row.
All inputs are finite; a program needn't handle non-finite values.
Results may differ from a plain program's by a relative error of at most 0.001.
Values may be sent and summed in bfloat16 or wider, within the bound.
A program may use at most 64 MiB of HBM per device.

v0:
```python
import jax
import jax.numpy as jnp
from jax import lax
from jax.sharding import PartitionSpec as P

BLOCK = 128


def joined_along(parts, dim):
    parts = jnp.moveaxis(parts, 0, dim)
    shape = parts.shape
    return parts.reshape(*shape[:dim], shape[dim] * shape[dim + 1], *shape[dim + 2 :])


def sent_to_all(x, axis):
    size = lax.axis_size(axis)
    return lax.all_to_all(jnp.broadcast_to(x[None], (size, *x.shape)), axis, 0, 0, tiled=True)


def gather_directly(x, axis, dim):
    return joined_along(sent_to_all(x, axis), dim)


def split_up(x, dim, size):
    shape = x.shape
    parts = x.reshape(*shape[:dim], size, shape[dim] // size, *shape[dim + 1 :])
    return jnp.moveaxis(parts, dim, 0)


def summed_on_arrival(x, axis, dim):
    size = lax.axis_size(axis)
    parts = lax.all_to_all(split_up(x, dim, size), axis, 0, 0, tiled=True)
    return jnp.sum(parts, axis=0)


def masked_tile(weight_tile, mask_tile):
    rows = weight_tile.shape[0]
    cols = weight_tile.shape[1]
    shaped = weight_tile.reshape(rows // BLOCK, BLOCK, cols // BLOCK, BLOCK)
    factor = mask_tile.astype(jnp.bfloat16)[:, None, :, None]
    return (shaped * factor).reshape(rows, cols)


def per_device(grad_output, inputs, weight, block_mask):
    grads_all = lax.all_gather(grad_output, "col", axis=0, tiled=True)
    inputs_all = gather_directly(inputs, "row", 0)
    tile_cols = weight.shape[1] // BLOCK
    mask_tile = lax.dynamic_slice_in_dim(
        block_mask, lax.axis_index("row") * tile_cols, tile_cols, 1
    )
    kept_tile = masked_tile(weight, mask_tile)
    partial_value = lax.dot_general(
        grads_all, kept_tile, (((1,), (1,)), ((), ())), preferred_element_type=jnp.float32
    )
    grad_input = summed_on_arrival(partial_value, "row", 0).astype(jnp.bfloat16)
    product = lax.dot_general(
        inputs_all, grads_all, (((0,), (0,)), ((), ())), preferred_element_type=jnp.float32
    )
    rows = product.shape[0]
    cols = product.shape[1]
    factor = mask_tile.astype(jnp.float32)[:, None, :, None]
    grad_weight = (
        (product.reshape(rows // BLOCK, BLOCK, cols // BLOCK, BLOCK) * factor)
        .reshape(rows, cols)
        .astype(jnp.bfloat16)
    )
    return (grad_input, grad_weight)


def solution(mesh):
    return jax.shard_map(
        per_device,
        mesh=mesh,
        in_specs=(P("col", "row"), P("row", "col"), P("col", "row"), P("col", None)),
        out_specs=(P("row", "col"), P("col", "row")),
        check_vma=False,
    )
```

profile of v0, /device:TPU:1, one launch (start us, length us, event | category | flops | bytes accessed | tf_op | source)
XLA Modules:
  0.0 135.1 jit_solution(849341611892757135)
XLA Ops:
  7.2 0.0 all-gather.2.cloned.1.call-start
  7.2 0.7 all-gather.2.cloned.1.call-update
  7.9 1.1 copy.19
  9.0 1.5 %broadcast_in_dim.2 = bf16[8,128,896]{1,2,0:T(8,128)(2,1)} broadcast(bf16[128,896]{0,1:T(8,128)(2,1)S(1)} %copy.19), dimensions={1,2} | broadcast | bytes 2064384 | tf_op jit(solution)/shard_map/broadcast_in_dim | solution.py:17
  10.5 0.0 copy-start.1
  10.5 6.5 %all-to-all-start.1 = ((bf16[8,128,896]{1,2,0:T(8,128)(2,1)}), bf16[8,128,896]{1,2,0:T(8,128)(2,1)S(1)}, u32[]{:S(2)}, u32[]{:S(2)}) async-start(bf16[8,128,896]{1,2,0:T(8,128)(2,1)} %broadcast_in_dim.2), calls=%async_computation.1 | async-start | bytes 3670016 | tf_op jit(solution)/shard_map/all_to_all | solution.py:17
  17.0 0.0 copy-done.1
  17.0 0.1 dynamic-slice_convert_fusion
  17.1 52.6 %all-gather.2.cloned.1.call-done = bf16[1024,1024]{1,0:T(8,128)(2,1)} async-done(((bf16[32,1024]{1,0:T(8,128)(2,1)}), bf16[1024,1024]{1,0:T(8,128)(2,1)}) %all-gather.2.cloned.1.call-update) | async-done | bytes 2097168 | tf_op jit(solution)/shard_map/all_gather | solution.py:45
  69.7 0.0 copy-start.2
  69.7 0.3 mul.23
  70.0 1.2 copy-done.2
  71.2 3.7 %convolution_bitcast_fusion = f32[112,8,8,128]{3,2,1,0:T(8,128)S(1)} fusion(bf16[1024,1024]{1,0:T(8,128)(2,1)} %all-gather.2.cloned.1.call-done, bf16[896,1024]{1,0:T(8,128)(2,1)S(1)} %copy-done.2, bf16[112,8,8,128]{3,2,1,0:T(8,128)(2,1)S(1)} %bitcast.38), kind=kOutput, calls=%fused_computation.2 | convolution fusion | flops 1879965696 | bytes 9437184 | tf_op jit(solution)/shard_map/dot_general | solution.py:52
  74.9 2.1 %copy.36 = f32[112,8,8,128]{3,2,0,1:T(8,128)} copy(f32[112,8,8,128]{3,2,1,0:T(8,128)S(1)} %convolution_bitcast_fusion) | data formatting | bytes 7340032 | tf_op jit(solution)/shard_map/reshape | solution.py:26
  77.0 0.0 all-to-all-done.1
  77.0 4.5 %all-to-all-start = ((f32[8,128,896]{1,2,0:T(8,128)}), f32[8,128,896]{1,2,0:T(8,128)}, u32[]{:S(2)}, u32[]{:S(2)}) async-start(f32[8,128,896]{1,2,0:T(8,128)} %bitcast.31), calls=%async_computation | async-start | bytes 7340032 | tf_op jit(solution)/shard_map/all_to_all | solution.py:32
  81.5 2.6 %copy.20 = bf16[8,128,896]{2,1,0:T(8,128)(2,1)} copy(bf16[8,128,896]{1,2,0:T(8,128)(2,1)S(1)} %all-to-all-done.1) | data formatting | bytes 3670016 | tf_op jit(solution)/shard_map/all_to_all | solution.py:17
  84.1 0.0 copy-start
  84.1 4.0 %copy.21 = bf16[896,1024]{1,0:T(8,128)(2,1)} copy(bf16[896,1024]{0,1:T(8,128)(2,1)} %bitcast.32) | data formatting | bytes 3670016 | tf_op jit(solution)/shard_map/dot_general | solution.py:56
  88.1 0.0 copy-done
  88.1 2.6 %copy.22 = bf16[1024,1024]{1,0:T(8,128)(2,1)} copy(bf16[1024,1024]{0,1:T(8,128)(2,1)S(1)} %bitcast.34) | data formatting | bytes 4194304 | tf_op jit(solution)/shard_map/dot_general | solution.py:56
  90.7 4.2 %multiply_convert_fusion = bf16[7,128,8,128]{3,1,2,0:T(8,128)(2,1)S(1)} fusion(bf16[7,128,1024,1]{2,1,3,0:T(8,128)(2,1)} %bitcast.37, bf16[8,128,1024,1]{2,1,0,3:T(8,128)(2,1)} %bitcast.35, f32[7,8]{1,0:T(8,128)S(1)} %get-tuple-element.6), kind=kOutput, calls=%fused_computation.1 | convolution fusion | flops 1880883200 | bytes 5767392 | tf_op jit(solution)/shard_map/dot_general | solution.py:56
  95.0 1.2 copy.23
  96.2 1.8 %copy.37 = bf16[112,8,8,128]{3,1,2,0:T(8,128)(2,1)} copy(bf16[112,8,8,128]{3,2,1,0:T(8,128)(2,1)S(1)} %bitcast.33) | data formatting | bytes 3670016
  97.9 27.2 %all-to-all-done = f32[8,128,896]{1,2,0:T(8,128)} async-done(((f32[8,128,896]{1,2,0:T(8,128)}), f32[8,128,896]{1,2,0:T(8,128)}, u32[]{:S(2)}, u32[]{:S(2)}) %all-to-all-start) | async-done | bytes 3670048 | tf_op jit(solution)/shard_map/all_to_all | solution.py:32
  125.2 2.2 %reduce_sum.9 = bf16[128,896]{0,1:T(8,128)(2,1)S(1)} reduce(f32[8,128,896]{1,2,0:T(8,128)} %all-to-all-done, f32[]{:T(128)} %constant.13.clone.1), dimensions={0}, to_apply=%region_0.0 | reduce | flops 802816 | bytes 3899396 | tf_op jit(solution)/shard_map/reduce_sum | solution.py:33
  127.4 0.8 copy.24
Async XLA Ops:
  7.2 62.5 %all-gather.2.cloned.1.call-start = ((), (), s32[]{:S(2)}) async-start(), calls=%async_computation.2 | async-start | bytes 2162688 | tf_op jit(solution)/shard_map/all_gather | solution.py:45
  10.5 6.5 %copy-start.1 = (s32[7,64]{1,0:T(8,128)S(1)}, s32[7,64]{1,0:T(8,128)}, u32[]{:S(2)}) copy-start(s32[7,64]{1,0:T(8,128)} %param.7) | copy-start | bytes 5380
  10.5 66.5 %all-to-all-start.1 = ((bf16[8,128,896]{1,2,0:T(8,128)(2,1)}), bf16[8,128,896]{1,2,0:T(8,128)(2,1)S(1)}, u32[]{:S(2)}, u32[]{:S(2)}) async-start(bf16[8,128,896]{1,2,0:T(8,128)(2,1)} %broadcast_in_dim.2), calls=%async_computation.1 | async-start | bytes 3670016 | tf_op jit(solution)/shard_map/all_to_all | solution.py:17
  69.7 1.5 %copy-start.2 = (bf16[896,1024]{1,0:T(8,128)(2,1)S(1)}, bf16[896,1024]{1,0:T(8,128)(2,1)}, u32[]{:S(2)}) copy-start(bf16[896,1024]{1,0:T(8,128)(2,1)} %param.6) | copy-start | bytes 5505028
  77.0 48.2 %all-to-all-start = ((f32[8,128,896]{1,2,0:T(8,128)}), f32[8,128,896]{1,2,0:T(8,128)}, u32[]{:S(2)}, u32[]{:S(2)}) async-start(f32[8,128,896]{1,2,0:T(8,128)} %bitcast.31), calls=%async_computation | async-start | bytes 7340032 | tf_op jit(solution)/shard_map/all_to_all | solution.py:32
  84.1 4.0 %copy-start = (bf16[1024,1024]{1,0:T(8,128)(2,1)S(1)}, bf16[1024,1024]{1,0:T(8,128)(2,1)}, u32[]{:S(2)}) copy-start(bf16[1024,1024]{1,0:T(8,128)(2,1)} %all-gather.2.cloned.1.call-done) | copy-start | bytes 6291460
Sparse Core Ops, SparseCore 0:
  10.5 59.1 all-gather.1
where the time goes:
time: 135 us
  waiting for transfers between devices  80.5 us (60%)
  local copies, waits for them, and re-layouts  19.1 us (14%)
  between operations  14.1 us (10%)
  starting transfers between devices  11 us (8%)
  matrix products  7.99 us (6%)
  other arithmetic  2.3 us (2%)
    all_gather x1, waiting for transfers between devices, per_device(): grads_all = lax.all_gather(grad_output, 'col', axis=0, tiled=True)  52.6 us
    all_to_all x1, waiting for transfers between devices, summed_on_arrival(): parts = lax.all_to_all(split_up(x, dim, size), axis, 0, 0, tiled=True)  27.2 us
    dot_general x2, local copies, waits for them, and re-layouts, per_device(): lax.dot_general(inputs_all, grads_all, (((0,), (0,)), ((), ())), preferre...  6.57 us
    all_to_all x1, starting transfers between devices, sent_to_all(): lax.all_to_all(jnp.broadcast_to(x[None], (size, *x.shape)), axis, 0, 0, t...  6.49 us
    unnamed x9, local copies, waits for them, and re-layouts  4.9 us
    all_to_all x1, starting transfers between devices, summed_on_arrival(): parts = lax.all_to_all(split_up(x, dim, size), axis, 0, 0, tiled=True)  4.5 us
    dot_general x1, matrix products, per_device(): lax.dot_general(inputs_all, grads_all, (((0,), (0,)), ((), ())), preferre...  4.25 us
    dot_general x1, matrix products, per_device(): lax.dot_general(grads_all, kept_tile, (((1,), (1,)), ((), ())), preferred...  3.75 us
  transfers between devices with their start and end apart: 3, of which 2 were waited for; matrix products, arithmetic and copies ran while one was open for 19% of the time, Pallas kernels for 0%

commit v1 on v0

--- a/solution.py
+++ b/solution.py
@@ -42,7 +42,16 @@
 
 
 def per_device(grad_output, inputs, weight, block_mask):
-    grads_all = lax.all_gather(grad_output, "col", axis=0, tiled=True)
+
+    def state_trace(work_x, which_axis):
+        return jnp.concatenate(
+            lax.all_to_all(
+                jnp.stack([work_x for _ in range(lax.psum(1, which_axis))]), which_axis, 0, 0
+            ),
+            axis=0,
+        )
+
+    grads_all = state_trace(grad_output, which_axis="col")
     inputs_all = gather_directly(inputs, "row", 0)
     tile_cols = weight.shape[1] // BLOCK
     mask_tile = lax.dynamic_slice_in_dim(

time: 135 us -> 149 us (1.10)
  between operations: 14.1 us -> 0.71 us
  starting transfers between devices: 11 us -> 24.2 us
  waiting for transfers between devices: 80.5 us -> 92.5 us
  local copies, waits for them, and re-layouts: 19.1 us -> 21.6 us
  matrix products: 7.99 us -> 6.39 us
    all_gather x1 -> x0, waiting for transfers between devices: 52.6 us -> none  [per_device(): grads_all = lax.all_gather(grad_output, 'col', axis=0, tiled=True)]
    all_to_all x0 -> x1, waiting for transfers between devices: none -> 49.4 us  [state_trace(): lax.all_to_all(jnp.stack([work_x for _ in range(lax.psum(1, which_axis))]...]
    all_to_all x1, waiting for transfers between devices: 0.01 us -> 18 us  [sent_to_all(): lax.all_to_all(jnp.broadcast_to(x[None], (size, *x.shape)), axis, 0, 0, t...]
    all_to_all x0 -> x1, starting transfers between devices: none -> 12.7 us  [state_trace(): lax.all_to_all(jnp.stack([work_x for _ in range(lax.psum(1, which_axis))]...]
    another operation x0 -> x1, local copies, waits for them, and re-layouts: none -> 2.45 us  [state_trace(): jnp.stack([work_x for _ in range(lax.psum(1, which_axis))])]
    all_to_all x1, waiting for transfers between devices: 27.2 us -> 25.1 us  [summed_on_arrival(): parts = lax.all_to_all(split_up(x, dim, size), axis, 0, 0, tiled=True)]
    dot_general x1, matrix products: 3.75 us -> 2.15 us  [per_device(): lax.dot_general(grads_all, kept_tile, (((1,), (1,)), ((), ())), preferred...]
  transfers between devices with their start and end apart: 3 -> 3, of which waited for: 2 -> 3; matrix products, arithmetic and copies ran while one was open for 19% -> 15% of each run, Pallas kernels for 0% -> 0%
where the time goes in v1:
time: 149 us; the launch traced here: 148 us
  waiting for transfers between devices  92.5 us (62%)
  starting transfers between devices  24.2 us (16%)
  local copies, waits for them, and re-layouts  21.6 us (14%)
  matrix products  6.39 us (4%)
  other arithmetic  2.3 us (2%)
    all_to_all x1, waiting for transfers between devices, state_trace(): lax.all_to_all(jnp.stack([work_x for _ in range(lax.psum(1, which_axis))]...  49.4 us
    all_to_all x1, waiting for transfers between devices, summed_on_arrival(): parts = lax.all_to_all(split_up(x, dim, size), axis, 0, 0, tiled=True)  25.1 us
    all_to_all x1, waiting for transfers between devices, sent_to_all(): lax.all_to_all(jnp.broadcast_to(x[None], (size, *x.shape)), axis, 0, 0, t...  18 us
    all_to_all x1, starting transfers between devices, state_trace(): lax.all_to_all(jnp.stack([work_x for _ in range(lax.psum(1, which_axis))]...  12.7 us
    all_to_all x1, starting transfers between devices, sent_to_all(): lax.all_to_all(jnp.broadcast_to(x[None], (size, *x.shape)), axis, 0, 0, t...  7.02 us
    dot_general x2, local copies, waits for them, and re-layouts, per_device(): lax.dot_general(inputs_all, grads_all, (((0,), (0,)), ((), ())), preferre...  6.4 us
    all_to_all x1, starting transfers between devices, summed_on_arrival(): parts = lax.all_to_all(split_up(x, dim, size), axis, 0, 0, tiled=True)  4.49 us
    dot_general x1, matrix products, per_device(): lax.dot_general(inputs_all, grads_all, (((0,), (0,)), ((), ())), preferre...  4.25 us
  transfers between devices with their start and end apart: 3, of which 3 were waited for; matrix products, arithmetic and copies ran while one was open for 15% of the time, Pallas kernels for 0%

profile of v1, /device:TPU:1, one launch (start us, length us, event | category | flops | bytes accessed | tf_op | source)
XLA Modules:
  0.0 147.7 jit_solution(18443043076820855471)
XLA Ops:
  0.6 2.5 %stack.2 = bf16[32,32,1024]{2,1,0:T(8,128)(2,1)} broadcast(bf16[32,1024]{1,0:T(8,128)(2,1)} %param.4), dimensions={1,2} | broadcast | bytes 2162688 | tf_op jit(solution)/shard_map/stack | solution.py:49
  3.1 0.0 copy-start
  3.1 12.7 %all-to-all-start = ((bf16[32,32,1024]{2,1,0:T(8,128)(2,1)}), bf16[32,32,1024]{2,1,0:T(8,128)(2,1)S(1)}, u32[]{:S(2)}, u32[]{:S(2)}) async-start(bf16[32,32,1024]{2,1,0:T(8,128)(2,1)} %stack.2), calls=%async_computation | async-start | bytes 4194304 | tf_op jit(solution)/shard_map/all_to_all | solution.py:48
  15.8 0.0 copy-done
  15.8 0.2 copy.19
  16.0 49.4 %all-to-all-done = bf16[32,32,1024]{2,1,0:T(8,128)(2,1)S(1)} async-done(((bf16[32,32,1024]{2,1,0:T(8,128)(2,1)}), bf16[32,32,1024]{2,1,0:T(8,128)(2,1)S(1)}, u32[]{:S(2)}, u32[]{:S(2)}) %all-to-all-start) | async-done | bytes 2097184 | tf_op jit(solution)/shard_map/all_to_all | solution.py:48
  65.4 1.5 broadcast_in_dim.2
  66.9 0.0 copy-start.1
  66.9 7.0 %all-to-all-start.2 = ((bf16[8,128,896]{1,2,0:T(8,128)(2,1)}), bf16[8,128,896]{1,2,0:T(8,128)(2,1)}, u32[]{:S(2)}, u32[]{:S(2)}) async-start(bf16[8,128,896]{1,2,0:T(8,128)(2,1)} %broadcast_in_dim.2), calls=%async_computation.2 | async-start | bytes 3670016 | tf_op jit(solution)/shard_map/all_to_all | solution.py:17
  73.9 0.0 copy-done.1
  73.9 0.0 copy-start.2
  73.9 0.1 dynamic-slice_convert_fusion
  74.0 0.3 mul.23
  74.3 1.1 copy-done.2
  75.4 2.1 %convolution_bitcast_fusion = f32[112,8,8,128]{3,2,1,0:T(8,128)S(1)} fusion(bf16[1024,1024]{1,0:T(8,128)(2,1)S(1)} %bitcast.34, bf16[896,1024]{1,0:T(8,128)(2,1)S(1)} %copy-done.2, bf16[112,8,8,128]{3,2,1,0:T(8,128)(2,1)S(1)} %bitcast.41), kind=kOutput, calls=%fused_computation.2 | convolution fusion | flops 1879965696 | bytes 9437184 | tf_op jit(solution)/shard_map/dot_general | solution.py:61
  77.6 2.1 %copy.36 = f32[112,8,8,128]{3,2,0,1:T(8,128)} copy(f32[112,8,8,128]{3,2,1,0:T(8,128)S(1)} %convolution_bitcast_fusion) | data formatting | bytes 7340032 | tf_op jit(solution)/shard_map/reshape | solution.py:26
  79.6 18.0 %all-to-all-done.2 = bf16[8,128,896]{1,2,0:T(8,128)(2,1)} async-done(((bf16[8,128,896]{1,2,0:T(8,128)(2,1)}), bf16[8,128,896]{1,2,0:T(8,128)(2,1)}, u32[]{:S(2)}, u32[]{:S(2)}) %all-to-all-start.2) | async-done | bytes 1835040 | tf_op jit(solution)/shard_map/all_to_all | solution.py:17
  97.6 4.5 %all-to-all-start.1 = ((f32[8,128,896]{1,2,0:T(8,128)}), f32[8,128,896]{1,2,0:T(8,128)}, u32[]{:S(2)}, u32[]{:S(2)}) async-start(f32[8,128,896]{1,2,0:T(8,128)} %bitcast.33), calls=%async_computation.1 | async-start | bytes 7340032 | tf_op jit(solution)/shard_map/all_to_all | solution.py:32
  102.1 3.8 %copy.20 = bf16[8,128,896]{2,1,0:T(8,128)(2,1)} copy(bf16[8,128,896]{1,2,0:T(8,128)(2,1)} %all-to-all-done.2) | data formatting | bytes 3670016 | tf_op jit(solution)/shard_map/all_to_all | solution.py:17
  105.9 3.8 %copy.21 = bf16[896,1024]{1,0:T(8,128)(2,1)} copy(bf16[896,1024]{0,1:T(8,128)(2,1)} %bitcast.36) | data formatting | bytes 3670016 | tf_op jit(solution)/shard_map/dot_general | solution.py:65
  109.7 2.6 %copy.22 = bf16[1024,1024]{1,0:T(8,128)(2,1)} copy(bf16[1024,1024]{0,1:T(8,128)(2,1)S(1)} %bitcast.35) | data formatting | bytes 4194304 | tf_op jit(solution)/shard_map/dot_general | solution.py:65
  112.3 4.2 %multiply_convert_fusion = bf16[7,128,8,128]{3,1,2,0:T(8,128)(2,1)S(1)} fusion(bf16[7,128,1024,1]{2,1,3,0:T(8,128)(2,1)} %bitcast.40, bf16[8,128,1024,1]{2,1,0,3:T(8,128)(2,1)} %bitcast.38, f32[7,8]{1,0:T(8,128)S(1)} %get-tuple-element.6), kind=kOutput, calls=%fused_computation.1 | convolution fusion | flops 1880883200 | bytes 5767392 | tf_op jit(solution)/shard_map/dot_general | solution.py:65
  116.6 1.2 copy.23
  117.8 1.8 %copy.37 = bf16[112,8,8,128]{3,1,2,0:T(8,128)(2,1)} copy(bf16[112,8,8,128]{3,2,1,0:T(8,128)(2,1)S(1)} %bitcast.37) | data formatting | bytes 3670016
  119.5 25.1 %all-to-all-done.1 = f32[8,128,896]{1,2,0:T(8,128)} async-done(((f32[8,128,896]{1,2,0:T(8,128)}), f32[8,128,896]{1,2,0:T(8,128)}, u32[]{:S(2)}, u32[]{:S(2)}) %all-to-all-start.1) | async-done | bytes 3670048 | tf_op jit(solution)/shard_map/all_to_all | solution.py:32
  144.6 2.2 %reduce_sum.9 = bf16[128,896]{0,1:T(8,128)(2,1)S(1)} reduce(f32[8,128,896]{1,2,0:T(8,128)} %all-to-all-done.1, f32[]{:T(128)} %constant.13.clone.1), dimensions={0}, to_apply=%region_0.0 | reduce | flops 802816 | bytes 3899396 | tf_op jit(solution)/shard_map/reduce_sum | solution.py:33
  146.8 0.8 copy.24
Async XLA Ops:
  3.1 12.7 %copy-start = (bf16[128,896]{1,0:T(8,128)(2,1)S(1)}, bf16[128,896]{1,0:T(8,128)(2,1)}, u32[]{:S(2)}) copy-start(bf16[128,896]{1,0:T(8,128)(2,1)} %param.5) | copy-start | bytes 688132
  3.1 62.3 %all-to-all-start = ((bf16[32,32,1024]{2,1,0:T(8,128)(2,1)}), bf16[32,32,1024]{2,1,0:T(8,128)(2,1)S(1)}, u32[]{:S(2)}, u32[]{:S(2)}) async-start(bf16[32,32,1024]{2,1,0:T(8,128)(2,1)} %stack.2), calls=%async_computation | async-start | bytes 4194304 | tf_op jit(solution)/shard_map/all_to_all | solution.py:48
  66.9 7.0 %copy-start.1 = (s32[7,64]{1,0:T(8,128)S(1)}, s32[7,64]{1,0:T(8,128)}, u32[]{:S(2)}) copy-start(s32[7,64]{1,0:T(8,128)} %param.7) | copy-start | bytes 5380
  66.9 30.8 %all-to-all-start.2 = ((bf16[8,128,896]{1,2,0:T(8,128)(2,1)}), bf16[8,128,896]{1,2,0:T(8,128)(2,1)}, u32[]{:S(2)}, u32[]{:S(2)}) async-start(bf16[8,128,896]{1,2,0:T(8,128)(2,1)} %broadcast_in_dim.2), calls=%async_computation.2 | async-start | bytes 3670016 | tf_op jit(solution)/shard_map/all_to_all | solution.py:17
  73.9 1.5 %copy-start.2 = (bf16[896,1024]{1,0:T(8,128)(2,1)S(1)}, bf16[896,1024]{1,0:T(8,128)(2,1)}, u32[]{:S(2)}) copy-start(bf16[896,1024]{1,0:T(8,128)(2,1)} %param.6) | copy-start | bytes 5505028
  97.6 47.0 %all-to-all-start.1 = ((f32[8,128,896]{1,2,0:T(8,128)}), f32[8,128,896]{1,2,0:T(8,128)}, u32[]{:S(2)}, u32[]{:S(2)}) async-start(f32[8,128,896]{1,2,0:T(8,128)} %bitcast.33), calls=%async_computation.1 | async-start | bytes 7340032 | tf_op jit(solution)/shard_map/all_to_all | solution.py:32
